TPU v7x, 512 devices: a whole 4x8x8 slice. The times are simulated.
512 devices in a mesh: req: 64 (over x, y_hi, z), tp: 8 (over y_lo, core).
Axes of the slice: x: 4, y: 8 (y_hi: 2, y_lo: 4; y = y_hi * 4 + y_lo), z: 8, core: 2. Of those that a mesh axis runs over, the one named last changes fastest.
Arguments:
- states: bfloat16 [64, 256, 1536], P('req', 'tp'), may hold values from -7 to 7
- gain_attn: bfloat16 [1536], replicated, may hold values from 0.25 to 1.75
- gain_moe: bfloat16 [1536], replicated, may hold values from 0.25 to 1.75
- w_query: bfloat16 [1536, 1536], P(None, 'tp'), may hold values from -4 to 4
- w_keyval: bfloat16 [1536, 1024], P(None, 'tp'), may hold values from -4 to 4
- w_out: bfloat16 [1536, 1536], P('tp'), may hold values from -0.875 to 0.875
- prefix_cache: bfloat16 [64, 128, 1024], P('req', None, 'tp'), may hold values from -6 to 6
- w_gate_up: bfloat16 [64, 1536, 512], P('req'), may hold values from -0.15625 to 0.15625
- w_down: bfloat16 [64, 256, 1536], P('req'), may hold values from -0.25 to 0.25
- routes: int32 [64, 256, 8], P('req', 'tp'), may hold values from 0 to 31, all different within a row; in each aligned block of 32 rows (0 to 31, 32 to 63, ..., all dimensions but the last counted through in order) at most 10 rows name the same one
- gates: float32 [64, 256, 8], P('req', 'tp'), may hold values from 0.05 to 0.3
- lengths: int32 [64], replicated, may hold values from 1 to 256, 14336 in all
- group_of: int32 [64], replicated, may hold values from 0 to 15
- owners: int32 [64], replicated, may hold values from 0 to 63, each once
Outputs:
- layer_out: bfloat16 [64, 256, 1536], P('req', 'tp')
Inputs may be any that keep to these rules, and one draw needn't show every extreme that they name: `routes`: in each aligned block of 32 rows (all leading dimensions taken together, in order) no expert is named by more than 10 rows, a bound that some block reaches. `owners`: each index of req appears once.
All inputs are finite; a program needn't handle non-finite values.
Results may differ from a plain program's by a relative error of at most 0.02.
Values may be sent and summed in bfloat16 or wider, within the bound.
No kernel may reach another device: no remote copies, remote signals or barrier semaphores. Data moves between devices by JAX's collectives and lax.ppermute only.
A program may use at most 64 MiB of HBM per device.

v0:
```python
import math
import jax
import jax.numpy as jnp
from jax import lax
from jax.sharding import PartitionSpec as P

D = 1536
HD = 64
EXPERTS = 32
TOPK = 8
PIECES = 4


def rms_scale(values, gain):
    spread = lax.rsqrt(jnp.mean(values * values, axis=-1, keepdims=True) + 1e-05)
    return values * spread * gain.astype(jnp.float32)


def apply_rotary(tensor, offset):
    count = tensor.shape[0]
    width = tensor.shape[-1] // 2
    place = offset + jnp.arange(count, dtype=jnp.float32)
    freq = jnp.exp(
        jnp.arange(width, dtype=jnp.float32) * (-2.0 * math.log(10000.0) / tensor.shape[-1])
    )
    angle = place[:, None] * freq[None, :]
    cosine = jnp.cos(angle)[:, None, :]
    sine = jnp.sin(angle)[:, None, :]
    first = tensor[..., :width]
    second = tensor[..., width:]
    return jnp.concatenate(
        [first * cosine - second * sine, second * cosine + first * sine], axis=-1
    )


def softmax_step(state, grouped, keys, values, keep):
    top, total, accum = state
    scores = jnp.einsum("hqd,khd->hqk", grouped, keys, preferred_element_type=jnp.float32) * (
        1.0 / math.sqrt(HD)
    )
    scores = jnp.where(keep, scores, -1e30)
    new_top = jnp.maximum(top, jnp.max(scores, axis=-1))
    weights = jnp.where(keep, jnp.exp(scores - new_top[..., None]), 0.0)
    fade = jnp.exp(top - new_top)
    total = total * fade + jnp.sum(weights, axis=-1)
    accum = accum * fade[..., None] + jnp.einsum(
        "hqk,khd->hqd", weights.astype(jnp.bfloat16), values, preferred_element_type=jnp.float32
    )
    return (new_top, total, accum)


def on_device(
    states,
    gain_attn,
    gain_moe,
    w_query,
    w_keyval,
    w_out,
    prefix_cache,
    w_gate_up,
    w_down,
    routes,
    gates,
    lengths,
    group_of,
    owners,
):
    devices_req = lax.axis_size("req")
    devices_tp = lax.axis_size("tp")
    mine = lax.axis_index("req")
    column = lax.axis_index("tp")
    local_rows = states.shape[1]
    full_rows = local_rows * devices_tp
    segment = prefix_cache.shape[1]
    plen = PIECES * segment
    length = lengths[mine]
    group = group_of[mine]
    resid_in = states[0].astype(jnp.float32)
    normed = rms_scale(resid_in, gain_attn).astype(jnp.bfloat16)
    gathered = lax.all_gather(normed, "tp", axis=0, tiled=True)
    q_heads = w_query.shape[1] // HD
    kv_heads = w_keyval.shape[1] // (2 * HD)
    per_kv = q_heads // kv_heads
    query_rows = jnp.dot(gathered, w_query, preferred_element_type=jnp.float32).reshape(
        full_rows, q_heads, HD
    )
    query_rows = apply_rotary(query_rows, float(plen)).astype(jnp.bfloat16)
    keyvals = jnp.dot(gathered, w_keyval, preferred_element_type=jnp.float32).reshape(
        full_rows, kv_heads, 2, HD
    )
    keys = apply_rotary(keyvals[:, :, 0], float(plen)).astype(jnp.bfloat16)
    values = keyvals[:, :, 1].astype(jnp.bfloat16)
    grouped = (
        query_rows.reshape(full_rows, kv_heads, per_kv, HD)
        .transpose(1, 2, 0, 3)
        .reshape(kv_heads, per_kv * full_rows, HD)
    )
    holder = jnp.arange(devices_req, dtype=jnp.int32)
    match = owners[None, :] == holder[:, None]
    piece_group = jnp.sum(jnp.where(match, holder[None, :], 0), axis=1) // PIECES
    start_state = (
        jnp.full((kv_heads, per_kv * full_rows), -1e30, jnp.float32),
        jnp.zeros((kv_heads, per_kv * full_rows), jnp.float32),
        jnp.zeros((kv_heads, per_kv * full_rows, HD), jnp.float32),
    )
    owned = piece_group == group

    def one_piece(state, inputs):
        block, flag = inputs
        block = block.reshape(segment, kv_heads, 2, HD)

        def update(inner_state):
            keep = jnp.ones((1, 1, segment), jnp.bool_)
            return softmax_step(inner_state, grouped, block[:, :, 0], block[:, :, 1], keep)

        return (lax.cond(flag, update, lambda inner_state: inner_state, state), None)

    result, unused = lax.scan(
        one_piece, start_state, (lax.all_gather(prefix_cache, "req", axis=0, tiled=True), owned)
    )
    state = result
    key_at = jnp.arange(full_rows)
    query_position = jnp.arange(per_kv * full_rows) % full_rows
    keep = (key_at[None, :] <= query_position[:, None]) & (key_at[None, :] < length)
    top, total, accum = softmax_step(state, grouped, keys, values, keep[None])
    mixed = (
        (accum / total[..., None]).reshape(kv_heads, per_kv, full_rows, HD).transpose(2, 0, 1, 3)
    )
    mixed = mixed.reshape(full_rows, q_heads * HD).astype(jnp.bfloat16)
    attended = lax.psum_scatter(
        jnp.dot(mixed, w_out, preferred_element_type=jnp.float32).astype(jnp.bfloat16),
        "tp",
        scatter_dimension=0,
        tiled=True,
    ).astype(jnp.float32)
    residual = resid_in + attended
    normed_moe = rms_scale(residual, gain_moe).astype(jnp.bfloat16)
    chosen = routes[0].reshape(-1)
    onehot = (chosen[:, None] == jnp.arange(EXPERTS, dtype=jnp.int32)[None, :]).astype(jnp.int32)
    slot_in = jnp.sum(jnp.cumsum(onehot, axis=0) * onehot, axis=1) - 1
    source = jnp.arange(chosen.shape[0], dtype=jnp.int32) // TOPK
    capacity = max(2, 5 * full_rows // (16 * devices_tp))
    outbound = (
        jnp.zeros((EXPERTS, capacity, D), jnp.bfloat16).at[chosen, slot_in].set(normed_moe[source])
    )
    slot_dev = 2 * EXPERTS // devices_req
    outgoing = jnp.repeat(outbound, 2, axis=0).reshape(devices_req, slot_dev, capacity, D)
    half_units = w_down.shape[1]
    pair = jnp.einsum(
        "nskd,sdf->nskf",
        lax.all_to_all(outgoing, "req", split_axis=0, concat_axis=0, tiled=True),
        w_gate_up,
        preferred_element_type=jnp.float32,
    )
    inner = (jax.nn.silu(pair[..., :half_units]) * pair[..., half_units:]).astype(jnp.bfloat16)
    produced = jnp.einsum(
        "nskf,sfd->nskd", inner, w_down, preferred_element_type=jnp.float32
    ).astype(jnp.bfloat16)
    returned = lax.all_to_all(produced, "req", split_axis=0, concat_axis=0, tiled=True)
    summed = jnp.sum(returned.reshape(EXPERTS, 2, capacity, D).astype(jnp.float32), axis=1).reshape(
        EXPERTS * capacity, D
    )
    selected_experts = summed[chosen * capacity + slot_in].reshape(local_rows, TOPK, D)
    expert_blend = jnp.einsum(
        "hv,hva->ha", gates[0], selected_experts, precision=lax.Precision.HIGHEST
    )
    row_at = column * local_rows + jnp.arange(local_rows)
    final = jnp.where((row_at < length)[:, None], residual + expert_blend, 0.0).astype(jnp.bfloat16)
    return final[None]


def solution(mesh):
    placed = (
        P("req", "tp", None),
        P(),
        P(),
        P(None, "tp"),
        P(None, "tp"),
        P("tp", None),
        P("req", None, "tp"),
        P("req", None, None),
        P("req", None, None),
        P("req", "tp", None),
        P("req", "tp", None),
        P(),
        P(),
        P(),
    )
    return jax.shard_map(
        on_device, mesh=mesh, in_specs=placed, out_specs=P("req", "tp", None), check_vma=False
    )
```

profile of v0, /device:TPU:1, one launch (start us, length us, event | category | flops | bytes accessed | tf_op | source)
XLA Modules:
  0.0 505.0 jit_solution(2194904492589218272)
XLA Ops:
  6.5 0.7 all-gather.2.cloned.1.call-update
  7.3 0.7 convert_element_type.106
  8.0 1.0 fusion.35
  9.3 1.0 fusion.37
  10.3 22.7 %all_gather.7 = bf16[256,1536]{1,0:T(8,128)(2,1)S(1)} all-gather(bf16[32,1536]{1,0:T(8,128)(2,1)S(1)} %fusion.37), channel_id=1, replica_groups=mesh['req'=64,'tp'=8] {'tp'}, dimensions={0}, use_global_device_ids=true | all-gather | bytes 884736 | tf_op jit(solution)/shard_map/all_gather | solution.py:80
  33.0 1.5 fusion.79
  34.7 0.7 copy.59
  35.6 0.7 dynamic_slice.16
  36.2 0.7 dynamic_slice.17
  36.9 0.6 iota_compare_fusion.4
  37.7 0.7 fusion.70
  39.0 1.3 fusion.78
  40.3 106.8 %all-gather.2.cloned.1.call-done = bf16[64,128,128]{2,1,0:T(8,128)(2,1)} async-done(((bf16[1,128,128]{2,1,0:T(8,128)(2,1)}), bf16[64,128,128]{2,1,0:T(8,128)(2,1)}) %all-gather.2.cloned.1.call-update) | async-done | bytes 2097168 | tf_op jit(solution)/shard_map/all_gather | solution.py:119
  147.1 4.1 copy.42
  151.3 87.6 %while.14 = (s32[]{:T(128)}, f32[1,768]{1,0:T(1,128)S(1)}, f32[1,768]{1,0:T(1,128)S(1)}, f32[1,768,64]{1,2,0:T(8,128)S(1)}, pred[64]{0:T(512)(128)(4,1)S(1)}, /*...) while((s32[]{:T(128)}, f32[1,768]{1,0:T(1,128)S(1)}, f32[1,768]{1,0:T(1,128)S(1)}, ...), condition=%wide.region_7.8_spmd, body=%wide.region_2.7_spmd.sunk | while | flops 25856260 | bytes 1922252 | solution.py:118
  152.6 0.6 dynamic_slice.20
  156.4 0.6 dynamic_slice.20
  158.9 1.4 conditional.2
  158.9 0.8 constant_dynamic-slice_fusion
  162.9 0.6 dynamic_slice.20
  191.1 1.4 conditional.2
  191.1 0.8 constant_dynamic-slice_fusion
  198.9 1.4 conditional.2
  198.9 0.8 constant_dynamic-slice_fusion
  215.7 1.4 conditional.2
  215.7 0.8 constant_dynamic-slice_fusion
  239.3 1.0 fusion.22
  240.3 1.0 convert_element_type.111
  241.3 1.3 convolution_convert_fusion.1
  242.9 0.6 reduce-window.6
  243.9 35.9 %reduce-scatter.2.cloned.1.call-done = bf16[32,1536]{1,0:T(8,128)(2,1)} async-done(((bf16[256,1536]{1,0:T(8,128)(2,1)}), bf16[32,1536]{1,0:T(8,128)(2,1)}) %reduce-scatter.2.cloned.1.call-update) | async-done | bytes 98320 | tf_op jit(solution)/shard_map/reduce_scatter | solution.py:130
  279.8 1.0 multiply_reduce_fusion
  280.9 1.0 multiply_convert_fusion
  281.9 1.3 gather_fusion
  283.2 19.5 %scatter_fusion = bf16[32,10,1536]{2,0,1:T(8,128)(2,1)S(1)} fusion(bf16[32,10,1536]{2,0,1:T(8,128)(2,1)S(1)} %broadcast_in_dim.99, s32[256]{0:T(256)S(1)} %bitcast.143, bf16[256,1536]{1,0:T(8,128)(2,1)S(1)} %gather_fusion), kind=kCustom, calls=%fused_computation.2 | custom fusion | bytes 2361344 | tf_op jit(solution)/shard_map/scatter | solution.py:144
  303.7 89.7 %all_to_all.10 = bf16[64,1,10,1536]{3,2,1,0:T(8,128)(2,1)S(1)} all-to-all(bf16[64,1,10,1536]{3,2,1,0:T(8,128)(2,1)S(1)} %bitcast.144), channel_id=1, replica_groups=mesh['req'=64,'tp'=8] {'req'}, dimensions={0} | all-to-all | bytes 3932160 | tf_op jit(solution)/shard_map/all_to_all | solution.py:151
  393.3 1.3 fusion.14
  394.6 0.7 fusion.7
  395.3 2.9 copy.50
  398.2 9.3 %all-to-all-start.1 = ((bf16[64,1,10,1536]{3,2,1,0:T(8,128)(2,1)}), bf16[64,1,10,1536]{3,2,1,0:T(8,128)(2,1)}, u32[]{:S(2)}, u32[]{:S(2)}) async-start(bf16[64,1,10,1536]{3,2,1,0:T(8,128)(2,1)} %copy.50), calls=%async_computation.2 | async-start | bytes 6291456 | tf_op jit(solution)/shard_map/all_to_all | solution.py:159
  407.7 1.2 add_compare_fusion
  408.8 0.6 pad_clamp_fusion
  409.4 75.0 %all-to-all-done.1 = bf16[64,1,10,1536]{3,2,1,0:T(8,128)(2,1)} async-done(((bf16[64,1,10,1536]{3,2,1,0:T(8,128)(2,1)}), bf16[64,1,10,1536]{3,2,1,0:T(8,128)(2,1)}, u32[]{:S(2)}, u32[]{:S(2)}) %all-to-all-start.1) | async-done | bytes 1966112 | tf_op jit(solution)/shard_map/all_to_all | solution.py:159
  484.4 4.8 convert_reduce_fusion
  489.2 2.0 reshape.446
  491.2 2.5 gather_fusion.1
  493.7 2.8 fusion.11
  496.5 1.7 fusion.44
  (209 shorter events, 43.0 us)
Async XLA Ops:
  6.5 386.8 %copy-start = (bf16[1,1536,512]{2,1,0:T(8,128)(2,1)S(1)}, bf16[1,1536,512]{2,1,0:T(8,128)(2,1)}, u32[]{:S(2)}) copy-start(bf16[1,1536,512]{2,1,0:T(8,128)(2,1)} %param.25) | copy-start | bytes 4718596
  6.5 140.6 %all-gather.2.cloned.1.call-start = ((), (), s32[]{:S(2)}) async-start(), calls=%async_computation.3 | async-start | bytes 2129920 | tf_op jit(solution)/shard_map/all_gather | solution.py:119
  7.3 272.6 %reduce-scatter.2.cloned.1.call-start = ((), (), s32[]{:S(2)}) async-start(), calls=%async_computation.4 | async-start | bytes 884736 | tf_op jit(solution)/shard_map/reduce_scatter | solution.py:130
  10.2 25.3 %copy-start.8 = (s32[64]{0:T(128)S(1)}, s32[64]{0:T(128)}, u32[]{:S(2)}) copy-start(s32[64]{0:T(128)} %param.29) | copy-start | bytes 772
  10.3 26.0 %copy-start.9 = (s32[64]{0:T(128)S(1)}, s32[64]{0:T(128)}, u32[]{:S(2)}) copy-start(s32[64]{0:T(128)} %param.30) | copy-start | bytes 772
  10.3 27.3 %copy-start.10 = (s32[64]{0:T(128)S(1)}, s32[64]{0:T(128)}, u32[]{:S(2)}) copy-start(s32[64]{0:T(128)} %param.31) | copy-start | bytes 772
  10.3 28.1 %copy-start.3 = (bf16[1536,128]{1,0:T(8,128)(2,1)S(1)}, bf16[1536,128]{1,0:T(8,128)(2,1)}, u32[]{:S(2)}) copy-start(bf16[1536,128]{1,0:T(8,128)(2,1)} %param.22) | copy-start | bytes 1179652
  238.9 2.3 copy-start.2
  239.2 3.3 copy-start.4
  239.2 3.7 copy-start.5
  240.2 39.6 %copy-start.1 = (bf16[1,32,1536]{2,1,0:T(8,128)(2,1)S(1)}, bf16[1,32,1536]{2,1,0:T(8,128)(2,1)}, u32[]{:S(2)}) copy-start(bf16[1,32,1536]{2,1,0:T(8,128)(2,1)} %param.18) | copy-start | bytes 294916
  393.3 1.3 copy-start.7
  398.2 9.3 %copy-start.6 = (f32[1,32,8]{1,2,0:T(8,128)S(1)}, f32[1,32,8]{1,2,0:T(8,128)}, u32[]{:S(2)}) copy-start(f32[1,32,8]{1,2,0:T(8,128)} %param.28) | copy-start | bytes 3076
  398.2 86.2 %all-to-all-start.1 = ((bf16[64,1,10,1536]{3,2,1,0:T(8,128)(2,1)}), bf16[64,1,10,1536]{3,2,1,0:T(8,128)(2,1)}, u32[]{:S(2)}, u32[]{:S(2)}) async-start(bf16[64,1,10,1536]{3,2,1,0:T(8,128)(2,1)} %copy.50), calls=%async_computation.2 | async-start | bytes 6291456 | tf_op jit(solution)/shard_map/all_to_all | solution.py:159
Sparse Core Ops, SparseCore 0:
  11.9 135.1 all-gather.1
  242.7 37.1 reduce-scatter.1
where the time goes:
time: 507 us; the launch traced here: 505 us
  waiting for transfers between devices  218 us (43%)
  blocking collectives  112 us (22%)
  local copies, waits for them, and re-layouts  77.9 us (15%)
  loops' own time  44.4 us (9%)
  other arithmetic  16.6 us (3%)
  between operations  13.8 us (3%)
  matrix products  12.2 us (2%)
  starting transfers between devices  9.38 us (2%)
    all_gather x1, waiting for transfers between devices, on_device(): lax.all_gather(prefix_cache, 'req', axis=0, tiled=True)  107 us
    all_to_all x1, blocking collectives, on_device(): lax.all_to_all(outgoing, 'req', split_axis=0, concat_axis=0, tiled=True)  89.7 us
    all_to_all x1, waiting for transfers between devices, on_device(): lax.all_to_all(produced, 'req', split_axis=0, concat_axis=0, tiled=True)  75 us
    another operation x1, loops' own time, on_device(): lax.scan(one_piece, start_state, (lax.all_gather(prefix_cache, 'req', axi...  43.3 us
    dynamic_slice x68, local copies, waits for them, and re-layouts, on_device(): lax.scan(one_piece, start_state, (lax.all_gather(prefix_cache, 'req', axi...  40.8 us
    reduce_scatter x1, waiting for transfers between devices, on_device(): lax.psum_scatter(jnp.dot(mixed, w_out, preferred_element_type=jnp.float32...  35.9 us
    all_gather x1, blocking collectives, on_device(): gathered = lax.all_gather(normed, 'tp', axis=0, tiled=True)  22.7 us
    scatter x2, local copies, waits for them, and re-layouts, on_device(): jnp.zeros((EXPERTS, capacity, D), jnp.bfloat16).at[chosen, slot_in]  20 us
  transfers between devices with their start and end apart: 3, of which 3 were waited for; matrix products, arithmetic and copies ran while one was open for 3% of the time, Pallas kernels for 0%

commit v1 on v0

--- a/solution.py
+++ b/solution.py
@@ -3,12 +3,26 @@
 import jax.numpy as jnp
 from jax import lax
 from jax.sharding import PartitionSpec as P
+from jax.lax import all_to_all, axis_size
 
 D = 1536
 HD = 64
 EXPERTS = 32
 TOPK = 8
 PIECES = 4
+
+
+def advance_stacks_all(z, across):
+    spare = jnp.concatenate(
+        all_to_all(
+            jnp.stack([z for _ in range(axis_size(across))], axis=0),
+            split_axis=0,
+            concat_axis=0,
+            axis_name=across,
+        ),
+        axis=0,
+    )
+    return spare
 
 
 def rms_scale(values, gain):
@@ -116,7 +130,7 @@
         return (lax.cond(flag, update, lambda inner_state: inner_state, state), None)
 
     result, unused = lax.scan(
-        one_piece, start_state, (lax.all_gather(prefix_cache, "req", axis=0, tiled=True), owned)
+        one_piece, start_state, (advance_stacks_all(prefix_cache, "req"), owned)
     )
     state = result
     key_at = jnp.arange(full_rows)

time: 507 us -> 448 us (0.88)
  waiting for transfers between devices: 218 us -> 111 us
  blocking collectives: 112 us -> 147 us
  starting transfers between devices: 9.38 us -> 29 us
    all_gather x1 -> x0, waiting for transfers between devices: 107 us -> none  [on_device(): lax.all_gather(prefix_cache, 'req', axis=0, tiled=True)]
    all_gather x1, blocking collectives: 22.7 us -> 57.4 us  [on_device(): gathered = lax.all_gather(normed, 'tp', axis=0, tiled=True)]
    all_to_all x0 -> x1, starting transfers between devices: none -> 20 us  [advance_stacks_all(): all_to_all(jnp.stack([z for _ in range(axis_size(across))], axis=0), spli...]
  transfers between devices with their start and end apart: 3 -> 3, of which waited for: 3 -> 2; matrix products, arithmetic and copies ran while one was open for 3% -> 2% of each run, Pallas kernels for 0% -> 0%
where the time goes in v1:
time: 448 us; the launch traced here: 445 us
  blocking collectives  147 us (33%)
  waiting for transfers between devices  111 us (25%)
  local copies, waits for them, and re-layouts  75.8 us (17%)
  loops' own time  42.6 us (10%)
  starting transfers between devices  29 us (6%)
  other arithmetic  14.1 us (3%)
  between operations  13.9 us (3%)
  matrix products  11.4 us (3%)
    all_to_all x1, blocking collectives, on_device(): lax.all_to_all(outgoing, 'req', split_axis=0, concat_axis=0, tiled=True)  89.7 us
    all_to_all x1, waiting for transfers between devices, on_device(): lax.all_to_all(produced, 'req', split_axis=0, concat_axis=0, tiled=True)  74.4 us
    all_gather x1, blocking collectives, on_device(): gathered = lax.all_gather(normed, 'tp', axis=0, tiled=True)  57.4 us
    another operation x1, loops' own time, on_device(): lax.scan(one_piece, start_state, (advance_stacks_all(prefix_cache, 'req')...  41.4 us
    dynamic_slice x68, local copies, waits for them, and re-layouts, on_device(): lax.scan(one_piece, start_state, (advance_stacks_all(prefix_cache, 'req')...  41.3 us
    reduce_scatter x1, waiting for transfers between devices, on_device(): lax.psum_scatter(jnp.dot(mixed, w_out, preferred_element_type=jnp.float32...  36.5 us
    scatter x2, local copies, waits for them, and re-layouts, on_device(): jnp.zeros((EXPERTS, capacity, D), jnp.bfloat16).at[chosen, slot_in]  20 us
    all_to_all x1, starting transfers between devices, advance_stacks_all(): all_to_all(jnp.stack([z for _ in range(axis_size(across))], axis=0), spli...  20 us
  transfers between devices with their start and end apart: 3, of which 2 were waited for; matrix products, arithmetic and copies ran while one was open for 2% of the time, Pallas kernels for 0%

profile of v1, /device:TPU:1, one launch (start us, length us, event | category | flops | bytes accessed | tf_op | source)
XLA Modules:
  0.0 444.7 jit_solution(1493313338891734780)
XLA Ops:
  6.5 1.0 copy.39
  7.5 1.8 stack.2
  9.3 20.0 %all-to-all-start = ((bf16[64,1,128,128]{2,3,1,0:T(8,128)(2,1)}), bf16[64,1,128,128]{2,3,1,0:T(8,128)(2,1)}, u32[]{:S(2)}, u32[]{:S(2)}) async-start(bf16[64,1,128,128]{2,3,1,0:T(8,128)(2,1)} %stack.2), calls=%async_computation | async-start | bytes 4194304 | tf_op jit(solution)/shard_map/all_to_all | solution.py:17
  29.9 57.4 %all_gather.3 = bf16[256,1536]{1,0:T(8,128)(2,1)S(1)} all-gather(bf16[32,1536]{1,0:T(8,128)(2,1)S(1)} %fusion.37), channel_id=1, replica_groups=mesh['req'=64,'tp'=8] {'tp'}, dimensions={0}, use_global_device_ids=true | all-gather | bytes 884736 | tf_op jit(solution)/shard_map/all_gather | solution.py:94
  89.5 0.6 iota_compare_fusion.4
  90.3 0.6 fusion.70
  90.9 1.4 fusion.80
  93.4 86.2 %while.14 = (s32[]{:T(128)}, f32[1,768]{1,0:T(1,128)S(1)}, f32[1,768]{1,0:T(1,128)S(1)}, f32[1,768,64]{1,2,0:T(8,128)S(1)}, pred[64]{0:T(512)(128)(4,1)S(1)}, /*...) while((s32[]{:T(128)}, f32[1,768]{1,0:T(1,128)S(1)}, f32[1,768]{1,0:T(1,128)S(1)}, ...), condition=%wide.region_7.8_spmd, body=%wide.region_2.7_spmd.sunk | while | flops 25856260 | bytes 1922252 | solution.py:132
  93.4 0.6 dynamic_slice.20
  94.7 0.6 dynamic_slice.20
  95.9 0.6 dynamic_slice.20
  97.2 0.6 dynamic_slice.20
  98.4 0.6 dynamic_slice.20
  99.7 0.6 dynamic_slice.20
  100.9 1.4 conditional.2
  100.9 0.8 constant_dynamic-slice_fusion
  102.4 0.6 dynamic_slice.20
  118.7 0.6 dynamic_slice.20
  122.5 0.6 dynamic_slice.20
  132.6 1.4 conditional.2
  132.6 0.8 constant_dynamic-slice_fusion
  140.3 1.4 conditional.2
  140.3 0.8 constant_dynamic-slice_fusion
  141.7 0.6 dynamic_slice.20
  145.5 0.6 dynamic_slice.20
  156.8 1.4 conditional.2
  156.8 0.8 constant_dynamic-slice_fusion
  162.0 0.6 dynamic_slice.20
  165.8 0.6 dynamic_slice.20
  180.0 1.2 fusion.22
  181.3 1.3 convolution_convert_fusion.1
  183.9 36.5 %reduce-scatter.2.cloned.1.call-done = bf16[32,1536]{1,0:T(8,128)(2,1)} async-done(((bf16[256,1536]{1,0:T(8,128)(2,1)}), bf16[32,1536]{1,0:T(8,128)(2,1)}) %reduce-scatter.2.cloned.1.call-update) | async-done | bytes 98320 | tf_op jit(solution)/shard_map/reduce_scatter | solution.py:144
  220.4 1.0 multiply_reduce_fusion
  221.5 1.0 multiply_convert_fusion
  222.5 1.3 gather_fusion
  223.8 19.5 %scatter_fusion = bf16[32,10,1536]{2,0,1:T(8,128)(2,1)S(1)} fusion(bf16[32,10,1536]{2,0,1:T(8,128)(2,1)S(1)} %broadcast_in_dim.99, s32[256]{0:T(256)S(1)} %bitcast.145, bf16[256,1536]{1,0:T(8,128)(2,1)S(1)} %gather_fusion), kind=kCustom, calls=%fused_computation.2 | custom fusion | bytes 2361344 | tf_op jit(solution)/shard_map/scatter | solution.py:158
  244.2 89.7 %all_to_all.15 = bf16[64,1,10,1536]{3,2,1,0:T(8,128)(2,1)S(1)} all-to-all(bf16[64,1,10,1536]{3,2,1,0:T(8,128)(2,1)S(1)} %bitcast.146), channel_id=1, replica_groups=mesh['req'=64,'tp'=8] {'req'}, dimensions={0} | all-to-all | bytes 3932160 | tf_op jit(solution)/shard_map/all_to_all | solution.py:165
  333.9 1.3 fusion.14
  335.2 0.7 fusion.7
  335.9 2.9 copy.50
  338.8 9.0 %all-to-all-start.2 = ((bf16[64,1,10,1536]{3,2,1,0:T(8,128)(2,1)}), bf16[64,1,10,1536]{3,2,1,0:T(8,128)(2,1)}, u32[]{:S(2)}, u32[]{:S(2)}) async-start(bf16[64,1,10,1536]{3,2,1,0:T(8,128)(2,1)} %copy.50), calls=%async_computation.3 | async-start | bytes 6291456 | tf_op jit(solution)/shard_map/all_to_all | solution.py:173
  347.9 1.2 add_compare_fusion
  349.7 74.4 %all-to-all-done.2 = bf16[64,1,10,1536]{3,2,1,0:T(8,128)(2,1)} async-done(((bf16[64,1,10,1536]{3,2,1,0:T(8,128)(2,1)}), bf16[64,1,10,1536]{3,2,1,0:T(8,128)(2,1)}, u32[]{:S(2)}, u32[]{:S(2)}) %all-to-all-start.2) | async-done | bytes 1966112 | tf_op jit(solution)/shard_map/all_to_all | solution.py:173
  424.1 4.8 %convert_reduce_fusion = f32[32,10,1536]{2,1,0:T(8,128)} fusion(bf16[32,2,10,1536]{3,2,1,0:T(8,128)(2,1)} %bitcast.142), kind=kLoop, calls=%fused_computation.18 | loop fusion | flops 1474560 | bytes 3932160 | tf_op jit(solution)/shard_map/reduce_sum | solution.py:174
  428.9 2.0 reshape.453
  430.9 2.5 gather_fusion.1
  433.4 2.8 fusion.11
  436.2 1.7 fusion.44
  (213 shorter events, 40.9 us)
Async XLA Ops:
  6.5 327.4 %copy-start = (bf16[1,1536,512]{2,1,0:T(8,128)(2,1)S(1)}, bf16[1,1536,512]{2,1,0:T(8,128)(2,1)}, u32[]{:S(2)}) copy-start(bf16[1,1536,512]{2,1,0:T(8,128)(2,1)} %param.25) | copy-start | bytes 4718596
  9.3 20.1 %copy-start.5 = (bf16[1536]{0:T(1024)(128)(2,1)S(1)}, bf16[1536]{0:T(1024)(128)(2,1)}, u32[]{:S(2)}) copy-start(bf16[1536]{0:T(1024)(128)(2,1)} %param.19) | copy-start | bytes 9220
  9.3 20.1 %copy-start.1 = (bf16[1,32,1536]{2,1,0:T(8,128)(2,1)S(1)}, bf16[1,32,1536]{2,1,0:T(8,128)(2,1)}, u32[]{:S(2)}) copy-start(bf16[1,32,1536]{2,1,0:T(8,128)(2,1)} %param.18) | copy-start | bytes 294916
  9.3 78.0 %copy-start.2 = (bf16[1536,192]{0,1:T(8,128)(2,1)S(1)}, bf16[1536,192]{0,1:T(8,128)(2,1)}, u32[]{:S(2)}) copy-start(bf16[1536,192]{0,1:T(8,128)(2,1)} %param.21) | copy-start | bytes 1769476
  9.3 84.0 %all-to-all-start = ((bf16[64,1,128,128]{2,3,1,0:T(8,128)(2,1)}), bf16[64,1,128,128]{2,3,1,0:T(8,128)(2,1)}, u32[]{:S(2)}, u32[]{:S(2)}) async-start(bf16[64,1,128,128]{2,3,1,0:T(8,128)(2,1)} %stack.2), calls=%async_computation | async-start | bytes 4194304 | tf_op jit(solution)/shard_map/all_to_all | solution.py:17
  29.3 191.1 %reduce-scatter.2.cloned.1.call-start = ((), (), s32[]{:S(2)}) async-start(), calls=%async_computation.4 | async-start | bytes 884736 | tf_op jit(solution)/shard_map/reduce_scatter | solution.py:144
  29.9 58.4 %copy-start.10 = (s32[64]{0:T(128)S(1)}, s32[64]{0:T(128)}, u32[]{:S(2)}) copy-start(s32[64]{0:T(128)} %param.29) | copy-start | bytes 772
  29.9 59.0 %copy-start.11 = (s32[64]{0:T(128)S(1)}, s32[64]{0:T(128)}, u32[]{:S(2)}) copy-start(s32[64]{0:T(128)} %param.30) | copy-start | bytes 772
  29.9 60.2 %copy-start.12 = (s32[64]{0:T(128)S(1)}, s32[64]{0:T(128)}, u32[]{:S(2)}) copy-start(s32[64]{0:T(128)} %param.31) | copy-start | bytes 772
  92.3 0.6 copy-start.4
  179.6 1.6 copy-start.3
  180.0 2.6 copy-start.6
  180.0 3.0 copy-start.7
  333.9 1.3 copy-start.9
  338.8 9.0 %copy-start.8 = (f32[1,32,8]{1,2,0:T(8,128)S(1)}, f32[1,32,8]{1,2,0:T(8,128)}, u32[]{:S(2)}) copy-start(f32[1,32,8]{1,2,0:T(8,128)} %param.28) | copy-start | bytes 3076
  338.8 85.3 %all-to-all-start.2 = ((bf16[64,1,10,1536]{3,2,1,0:T(8,128)(2,1)}), bf16[64,1,10,1536]{3,2,1,0:T(8,128)(2,1)}, u32[]{:S(2)}, u32[]{:S(2)}) async-start(bf16[64,1,10,1536]{3,2,1,0:T(8,128)(2,1)} %copy.50), calls=%async_computation.3 | async-start | bytes 6291456 | tf_op jit(solution)/shard_map/all_to_all | solution.py:173
Sparse Core Ops, SparseCore 0:
  182.7 37.6 reduce-scatter.1
